TPU v7x, 32 devices: a whole 2x2x4 slice. The times are simulated.
32 devices in a mesh: dp: 8 (over y, x, core), tensor: 4 (over z).
Axes of the slice: x: 2, y: 2, z: 4, core: 2. Of those that a mesh axis runs over, the one named last changes fastest.
Arguments:
- hidden_in: bfloat16 [16384, 1024], P('dp'), may hold values from -6 to 6
- lengths: int32 [8], P('dp'), may hold values from 512 to 2048, as said below
- query_weight: bfloat16 [1024, 1024], P(None, 'tensor'), may hold values from -0.1875 to 0.1875
- query_bias: bfloat16 [1024], P('tensor'), may hold values from -1 to 1
- key_weight: bfloat16 [1024, 1024], P(None, 'tensor'), may hold values from -0.1875 to 0.1875
- value_weight: bfloat16 [1024, 1024], P(None, 'tensor'), may hold values from -0.1875 to 0.1875
- value_bias: bfloat16 [1024], P('tensor'), may hold values from -1 to 1
- output_weight: bfloat16 [1024, 1024], P(None, 'tensor'), may hold values from -2 to 2
- output_bias: bfloat16 [1024], replicated, may hold values from -1 to 1
- first_gain: bfloat16 [1024], replicated, may hold values from 0.5 to 1.5
- first_shift: bfloat16 [1024], replicated, may hold values from -1 to 1
- inner_weight: bfloat16 [1024, 4096], P(None, 'tensor'), may hold values from -0.1875 to 0.1875
- inner_bias: bfloat16 [4096], P('tensor'), may hold values from -1 to 1
- outer_weight: bfloat16 [1024, 4096], P(None, 'tensor'), may hold values from -0.125 to 0.125
- outer_bias: bfloat16 [1024], replicated, may hold values from -1 to 1
- second_gain: bfloat16 [1024], replicated, may hold values from 0.5 to 1.5
- second_shift: bfloat16 [1024], replicated, may hold values from -1 to 1
- cotangent: bfloat16 [16384, 1024], P('dp'), may hold values from -6 to 6
- teacher: bfloat16 [16384, 1024], P('dp'), may hold values from -6 to 6
Outputs:
- layer_output: bfloat16 [16384, 1024], P(('dp', 'tensor'))
- distill_loss: float32 [], replicated
- input_grad: float32 [16384, 1024], P(('dp', 'tensor'))
- query_weight_grad: float32 [1024, 1024], P('dp', 'tensor')
- query_bias_grad: float32 [1024], replicated
- key_weight_grad: float32 [1024, 1024], P('dp', 'tensor')
- value_weight_grad: float32 [1024, 1024], P('dp', 'tensor')
- value_bias_grad: float32 [1024], replicated
- output_weight_grad: float32 [1024, 1024], P('dp', 'tensor')
- output_bias_grad: float32 [1024], replicated
- first_gain_grad: float32 [1024], replicated
- first_shift_grad: float32 [1024], replicated
- inner_weight_grad: float32 [1024, 4096], P('dp', 'tensor')
- inner_bias_grad: float32 [4096], replicated
- outer_weight_grad: float32 [1024, 4096], P('dp', 'tensor')
- outer_bias_grad: float32 [1024], replicated
- second_gain_grad: float32 [1024], replicated
- second_shift_grad: float32 [1024], replicated
Inputs may be any that keep to these rules, and one draw needn't show every extreme that they name: `lengths`: one sequence's valid tokens; slots after them are padding; some sequence fills all 2048 slots.
All inputs are finite; a program needn't handle non-finite values.
Results may differ from a plain program's by a relative error of at most 0.018.
Values may be sent and summed in bfloat16 or wider, within the bound.
No kernel may reach another device: no remote copies, remote signals or barrier semaphores. Data moves between devices by JAX's collectives and lax.ppermute only.
A program may use at most 256 MiB of HBM per device.

v0:
```python
import math
import jax
import jax.numpy as jnp
from jax import lax
from jax.sharding import PartitionSpec as P

HD = 64
epsilon = 1e-05


def matmul(former, latter):
    return jnp.dot(former, latter, preferred_element_type=jnp.float32)


def times_rows(former, latter):
    return lax.dot_general(
        former, latter, (((1,), (1,)), ((), ())), preferred_element_type=jnp.float32
    )


def over_rows(former, latter):
    return lax.dot_general(
        former, latter, (((0,), (0,)), ((), ())), preferred_element_type=jnp.float32
    )


def layer_norm(hidden, norm_gain, norm_shift):
    centered = hidden - jnp.mean(hidden, axis=-1, keepdims=True)
    inverse = lax.rsqrt(jnp.mean(centered * centered, axis=-1, keepdims=True) + epsilon)
    normal = centered * inverse
    return (normal * norm_gain + norm_shift, normal, inverse)


def norm_back(upstream, normal, inverse, norm_gain):
    scaled = upstream * norm_gain
    return inverse * (
        scaled
        - jnp.mean(scaled, axis=-1, keepdims=True)
        - normal * jnp.mean(scaled * normal, axis=-1, keepdims=True)
    )


def gelu_exact(values):
    return 0.5 * values * (1.0 + jax.scipy.special.erf(values * 0.7071067811865476))


def gelu_slope(values):
    return (
        0.5 * (1.0 + jax.scipy.special.erf(values * 0.7071067811865476))
        + values * jnp.exp(-0.5 * values * values) * 0.3989422804014327
    )


def split_blocks(queries, keys_all, values_all):
    seq_len, local_width = queries.shape
    heads_here = local_width // HD
    block_rows = min(512, seq_len)
    block_count = seq_len // block_rows
    keys_split = keys_all.reshape(seq_len, heads_here, HD)
    values_split = values_all.reshape(seq_len, heads_here, HD)
    query_blocks = queries.reshape(block_count, block_rows, heads_here, HD)
    return (keys_split, values_split, query_blocks, block_count, block_rows, heads_here)


def block_scores(query_block, keys_split, key_valid, score_scale):
    scores = (
        jnp.einsum("qhd,khd->hqk", query_block, keys_split, preferred_element_type=jnp.float32)
        * score_scale
    )
    return jnp.where(key_valid[None, None, :], scores, -1e30)


def attend_forward(queries, keys_all, values_all, key_valid, score_scale):
    keys_split, values_split, query_blocks, block_count, block_rows, heads_here = split_blocks(
        queries, keys_all, values_all
    )

    def one_block(query_block):
        scores = block_scores(query_block, keys_split, key_valid, score_scale)
        row_peak = jnp.max(scores, axis=-1, keepdims=True)
        exponent = jnp.exp(scores - row_peak)
        row_total = jnp.sum(exponent, axis=-1, keepdims=True)
        probs = (exponent / row_total).astype(jnp.bfloat16)
        context = jnp.einsum(
            "hqk,khd->qhd", probs, values_split, preferred_element_type=jnp.float32
        )
        return (context, (row_peak + jnp.log(row_total))[..., 0])

    context, logsum = lax.map(one_block, query_blocks)
    return (context.reshape(queries.shape), logsum)


def attend_backward(queries, keys_all, values_all, key_valid, score_scale, logsum, context_grad):
    keys_split, values_split, query_blocks, block_count, block_rows, heads_here = split_blocks(
        queries, keys_all, values_all
    )
    grad_blocks = context_grad.reshape(block_count, block_rows, heads_here, HD)

    def one_block(carry, inputs):
        key_sum, value_sum = carry
        query_block, grad_block, logsum_block = inputs
        scores = block_scores(query_block, keys_split, key_valid, score_scale)
        probs = jnp.exp(scores - logsum_block[..., None])
        prob_grad = jnp.einsum(
            "qhd,khd->hqk", grad_block, values_split, preferred_element_type=jnp.float32
        )
        centre = jnp.sum(probs * prob_grad, axis=-1, keepdims=True)
        score_grad = (probs * (prob_grad - centre)).astype(jnp.bfloat16)
        query_grad = (
            jnp.einsum("hqk,khd->qhd", score_grad, keys_split, preferred_element_type=jnp.float32)
            * score_scale
        )
        key_sum = (
            key_sum
            + jnp.einsum(
                "hqk,qhd->khd", score_grad, query_block, preferred_element_type=jnp.float32
            )
            * score_scale
        )
        value_sum = value_sum + jnp.einsum(
            "hqk,qhd->khd",
            probs.astype(jnp.bfloat16),
            grad_block,
            preferred_element_type=jnp.float32,
        )
        return ((key_sum, value_sum), query_grad)

    zero_block = jnp.zeros(keys_split.shape, jnp.float32)
    (key_sum, value_sum), query_grads = lax.scan(
        one_block, (zero_block, zero_block), (query_blocks, grad_blocks, logsum)
    )
    return (
        query_grads.reshape(queries.shape),
        key_sum.reshape(queries.shape),
        value_sum.reshape(queries.shape),
    )


def shards(
    hidden_in,
    lengths,
    query_weight,
    query_bias,
    key_weight,
    value_weight,
    value_bias,
    output_weight,
    output_bias,
    first_gain,
    first_shift,
    inner_weight,
    inner_bias,
    outer_weight,
    outer_bias,
    second_gain,
    second_shift,
    cotangent,
    teacher,
):
    seq_len, model_width = hidden_in.shape
    tensor_size = lax.axis_size("tensor")
    tensor_index = lax.axis_index("tensor")
    share_rows = seq_len // tensor_size
    row_start = tensor_index * share_rows
    score_scale = 1.0 / math.sqrt(HD)
    positions = jnp.arange(seq_len, dtype=jnp.int32)
    row_valid = positions < lengths[0]
    token_total = lax.psum(jnp.sum(lengths), "dp").astype(jnp.float32)
    grad_scale = seq_len * lax.axis_size("dp") / (2.0 * token_total)
    hidden_float = hidden_in.astype(jnp.float32)
    queries = (matmul(hidden_in, query_weight) + query_bias).astype(jnp.bfloat16)
    keys_all = matmul(hidden_in, key_weight).astype(jnp.bfloat16)
    values_all = (matmul(hidden_in, value_weight) + value_bias).astype(jnp.bfloat16)
    context, logsum = attend_forward(queries, keys_all, values_all, row_valid, score_scale)
    context_low = context.astype(jnp.bfloat16)
    attention_part = times_rows(context_low, output_weight)

    def take_own(array_in):
        return lax.dynamic_slice_in_dim(array_in, row_start, share_rows, 0)

    attention_whole = lax.psum(attention_part, "tensor")
    normed, normal_one, inverse_one = layer_norm(
        hidden_float + (attention_whole + output_bias), first_gain, first_shift
    )
    normed_low = normed.astype(jnp.bfloat16)
    inner = matmul(normed_low, inner_weight) + inner_bias
    activated = gelu_exact(inner).astype(jnp.bfloat16)
    outer_part = times_rows(activated, outer_weight)
    outer_rows = lax.psum(outer_part, "tensor")
    final, normal_two, inverse_two = layer_norm(
        normed + (outer_rows + outer_bias), second_gain, second_shift
    )
    row_mask = row_valid[:, None]
    difference = final - teacher.astype(jnp.float32)
    loss_part = jnp.sum(take_own(jnp.where(row_mask, difference * difference, 0.0)))
    final_grad = jnp.where(row_mask, cotangent.astype(jnp.float32) + grad_scale * difference, 0.0)
    second_grad = norm_back(final_grad, normal_two, inverse_two, second_gain)
    branch_low = second_grad.astype(jnp.bfloat16)
    activated_grad = matmul(branch_low, outer_weight)
    outer_weight_grad = over_rows(branch_low, activated)
    inner_low = (activated_grad * gelu_slope(inner)).astype(jnp.bfloat16)
    inner_bias_grad = jnp.sum(inner_low.astype(jnp.float32), axis=0)
    inner_weight_grad = over_rows(normed_low, inner_low)
    normed_part = times_rows(inner_low, inner_weight)
    normed_back = lax.psum(normed_part, "tensor")
    normed_grad = second_grad + normed_back
    first_grad = norm_back(normed_grad, normal_one, inverse_one, first_gain)
    attention_low = first_grad.astype(jnp.bfloat16)
    output_weight_grad = over_rows(attention_low, context_low)
    context_grad = matmul(attention_low, output_weight).astype(jnp.bfloat16)
    query_grad, key_grad, value_grad = attend_backward(
        queries, keys_all, values_all, row_valid, score_scale, logsum, context_grad
    )
    query_low = query_grad.astype(jnp.bfloat16)
    key_low = key_grad.astype(jnp.bfloat16)
    value_low = value_grad.astype(jnp.bfloat16)
    input_part = (
        times_rows(query_low, query_weight)
        + times_rows(key_low, key_weight)
        + times_rows(value_low, value_weight)
    )
    input_back = lax.psum(input_part.astype(jnp.bfloat16), "tensor").astype(jnp.float32)
    input_rows = take_own(input_back) + take_own(first_grad)
    weight_grads = (
        lax.psum_scatter(
            over_rows(hidden_in, query_low).astype(jnp.bfloat16),
            "dp",
            scatter_dimension=0,
            tiled=True,
        ).astype(jnp.float32),
        lax.psum_scatter(
            over_rows(hidden_in, key_low).astype(jnp.bfloat16),
            "dp",
            scatter_dimension=0,
            tiled=True,
        ).astype(jnp.float32),
        lax.psum_scatter(
            over_rows(hidden_in, value_low).astype(jnp.bfloat16),
            "dp",
            scatter_dimension=0,
            tiled=True,
        ).astype(jnp.float32),
        lax.psum_scatter(
            output_weight_grad.astype(jnp.bfloat16), "dp", scatter_dimension=0, tiled=True
        ).astype(jnp.float32),
        lax.psum_scatter(
            inner_weight_grad.astype(jnp.bfloat16), "dp", scatter_dimension=0, tiled=True
        ).astype(jnp.float32),
        lax.psum_scatter(
            outer_weight_grad.astype(jnp.bfloat16), "dp", scatter_dimension=0, tiled=True
        ).astype(jnp.float32),
    )

    def placed(vector_in):
        full_zeros = jnp.zeros((vector_in.shape[0] * tensor_size,), jnp.float32)
        return lax.dynamic_update_slice_in_dim(
            full_zeros, vector_in, tensor_index * vector_in.shape[0], 0
        )

    vector_grads = lax.psum(
        (
            placed(jnp.sum(query_low.astype(jnp.float32), axis=0)),
            placed(jnp.sum(value_low.astype(jnp.float32), axis=0)),
            jnp.sum(take_own(attention_low).astype(jnp.float32), axis=0),
            jnp.sum(take_own(normed_grad * normal_one), axis=0),
            jnp.sum(take_own(normed_grad), axis=0),
            placed(inner_bias_grad),
            jnp.sum(take_own(branch_low).astype(jnp.float32), axis=0),
            jnp.sum(take_own(final_grad * normal_two), axis=0),
            jnp.sum(take_own(final_grad), axis=0),
            loss_part,
        ),
        ("dp", "tensor"),
    )
    (
        query_bias_grad,
        value_bias_grad,
        output_bias_grad,
        first_gain_grad,
        first_shift_grad,
        inner_bias_full,
        outer_bias_grad,
        second_gain_grad,
        second_shift_grad,
        loss_total,
    ) = vector_grads
    (
        query_weight_grad,
        key_weight_grad,
        value_weight_grad,
        output_weight_sum,
        inner_weight_sum,
        outer_weight_sum,
    ) = weight_grads
    distill_loss = loss_total / token_total
    return (
        take_own(final).astype(jnp.bfloat16),
        distill_loss,
        input_rows,
        query_weight_grad,
        query_bias_grad,
        key_weight_grad,
        value_weight_grad,
        value_bias_grad,
        output_weight_sum,
        output_bias_grad,
        first_gain_grad,
        first_shift_grad,
        inner_weight_sum,
        inner_bias_full,
        outer_weight_sum,
        outer_bias_grad,
        second_gain_grad,
        second_shift_grad,
    )


def solution(mesh):
    in_specs = (
        P("dp", None),
        P("dp"),
        P(None, "tensor"),
        P("tensor"),
        P(None, "tensor"),
        P(None, "tensor"),
        P("tensor"),
        P(None, "tensor"),
        P(),
        P(),
        P(),
        P(None, "tensor"),
        P("tensor"),
        P(None, "tensor"),
        P(),
        P(),
        P(),
        P("dp", None),
        P("dp", None),
    )
    out_specs = (
        P(("dp", "tensor"), None),
        P(),
        P(("dp", "tensor"), None),
        P("dp", "tensor"),
        P(),
        P("dp", "tensor"),
        P("dp", "tensor"),
        P(),
        P("dp", "tensor"),
        P(),
        P(),
        P(),
        P("dp", "tensor"),
        P(),
        P("dp", "tensor"),
        P(),
        P(),
        P(),
    )
    return jax.shard_map(shards, mesh=mesh, in_specs=in_specs, out_specs=out_specs, check_vma=False)
```

profile of v0, /device:TPU:0, one launch (start us, length us, event | category | flops | bytes accessed | tf_op | source)
XLA Modules:
  0.0 1564.1 jit_solution(17279428161375169190)
XLA Ops:
  25.2 55.2 %while.28 = (s32[]{:T(128)}, bf16[4,512,4,64]{1,3,2,0:T(8,128)(2,1)}, f32[4,4,512]{2,1,0:T(4,128)S(1)}, bf16[4,512,4,64]{1,3,2,0:T(8,128)(2,1)}, bf16[2048,4,64]...) while((s32[]{:T(128)}, bf16[4,512,4,64]{1,3,2,0:T(8,128)(2,1)}, ...), condition=%wide.region_3.4_spmd.clone, body=%wide.region_0.3_spmd.clone.sunk | while | flops 1124073472 | bytes 65872064 | solution.py:89
  89.8 293.4 %all-reduce.6.cloned.1.call-done = f32[2048,1024]{1,0:T(8,128)} async-done(((f32[2048,1024]{1,0:T(8,128)}), f32[2048,1024]{1,0:T(8,128)}) %all-reduce.6.cloned.1.call-update) | async-done | bytes 8388624 | tf_op jit(solution)/shard_map/psum | solution.py:181
  394.8 7.4 multiply_convert_fusion.1
  404.1 6.9 fusion.71
  411.0 8.8 psum.108
  421.3 279.7 %all-reduce.8.cloned.1.call-done = f32[2048,1024]{1,0:T(8,128)} async-done(((f32[2048,1024]{1,0:T(8,128)}), f32[2048,1024]{1,0:T(8,128)}) %all-reduce.8.cloned.1.call-update) | async-done | bytes 8388624 | tf_op jit(solution)/shard_map/psum | solution.py:189
  708.8 10.9 multiply_reduce_fusion.6
  725.8 11.3 convert_reduce_fusion
  739.1 6.9 fusion.72
  746.5 9.4 convolution_convert_fusion.2
  756.0 10.5 convolution_convert_fusion.3
  766.7 269.2 %all-reduce.10.cloned.1.call-done = f32[2048,1024]{1,0:T(8,128)} async-done(((f32[2048,1024]{1,0:T(8,128)}), f32[2048,1024]{1,0:T(8,128)}) %all-reduce.10.cloned.1.call-update) | async-done | bytes 8388624 | tf_op jit(solution)/shard_map/psum | solution.py:205
  1036.0 16.3 %multiply_reduce_fusion.5 = (f32[2048]{0:T(1024)S(1)}, f32[2048]{0:T(1024)S(1)}, f32[2048,1024]{1,0:T(8,128)}) fusion(f32[1024]{0:T(1024)S(1)} %convert_element_type.183, f32[2048,1024]{1,0:T(8,128)} %copy-done.5, f32[2048,1024]{1,0:T(8,128)} %all-reduce.10.cloned.1.call-done, f32[2048,1024]{1,0:T(8,128)} %copy-done.7, f32[2048]{0:T(1024)S(1)} %get-tuple-element.345, ...), kind=kLoop, calls=%fused_computation.76 | loop fusion | flops 20967424 | bytes 41992192 | tf_op jit(solution)/shard_map/reduce_sum | solution.py:38
  1052.4 9.8 fusion.67
  1076.0 166.5 %while.29 = (s32[]{:T(128)}, f32[2048,4,64]{0,2,1:T(8,128)S(1)}, f32[2048,4,64]{0,2,1:T(8,128)}, bf16[4,512,4,64]{1,3,2,0:T(8,128)(2,1)}, bf16[4,512,4,64]{1,3,2...) while((s32[]{:T(128)}, f32[2048,4,64]{0,2,1:T(8,128)S(1)}, ...), condition=%wide.region_20.21_spmd.clone, body=%wide.region_18.20_spmd.clone.sunk | while | flops 2750021632 | bytes 180945136 | solution.py:129
  1086.7 10.1 multiply_reduce_fusion.8
  1096.8 11.0 multiply_convert_fusion.3
  1107.8 7.2 fusion.151
  1128.8 9.9 multiply_reduce_fusion.8
  1138.7 10.6 multiply_convert_fusion.3
  1149.3 7.1 fusion.151
  1170.2 9.9 multiply_reduce_fusion.8
  1180.1 10.6 multiply_convert_fusion.3
  1190.7 7.1 fusion.151
  1211.7 9.9 multiply_reduce_fusion.8
  1221.6 10.6 multiply_convert_fusion.3
  1232.2 7.1 fusion.151
  1277.1 9.1 add_convert_fusion
  1304.3 40.3 %all-reduce = (f32[]{:T(128)}, f32[1024]{0:T(1024)}, f32[1024]{0:T(1024)}, f32[1024]{0:T(1024)}, f32[1024]{0:T(1024)}, /*index=5*/f32[1024]{0:T(1024)}, f32[4096...) all-reduce(f32[]{:T(128)} %get-tuple-element.344, ...), channel_id=1, replica_groups=mesh['dp'=8,'tensor'=4] {'dp','tensor'}, use_global_device_ids=true, to_apply=%region_11.12 | all-reduce | flops 12289 | bytes 98312 | tf_op jit(solution)/shard_map/psum | solution.py:260
  1348.7 8.8 reduce-scatter.23.cloned.1.call-done
  1359.3 35.5 %reduce-scatter.13.cloned.1.call-done = bf16[128,256]{1,0:T(8,128)(2,1)} async-done(((bf16[1024,256]{1,0:T(8,128)(2,1)}), bf16[128,256]{1,0:T(8,128)(2,1)}) %reduce-scatter.13.cloned.1.call-update) | async-done | bytes 65552 | tf_op jit(solution)/shard_map/reduce_scatter | solution.py:243
  1396.3 155.7 %all-reduce.12.cloned.1.call-done = bf16[2048,1024]{1,0:T(8,128)(2,1)} async-done(((bf16[2048,1024]{1,0:T(8,128)(2,1)}), bf16[2048,1024]{1,0:T(8,128)(2,1)}) %all-reduce.12.cloned.1.call-update) | async-done | bytes 4194320 | tf_op jit(solution)/shard_map/psum | solution.py:222
  (257 shorter events, 243.7 us)
Async XLA Ops:
  7.2 387.5 %copy-start = (bf16[1024,1024]{1,0:T(8,128)(2,1)S(1)}, bf16[1024,1024]{1,0:T(8,128)(2,1)}, u32[]{:S(2)}) copy-start(bf16[1024,1024]{1,0:T(8,128)(2,1)} %param.34) | copy-start | bytes 6291460
  7.2 376.0 %all-reduce.6.cloned.1.call-start = ((), (), s32[]{:S(2)}) async-start(), calls=%async_computation.6 | async-start | bytes 16777216 | tf_op jit(solution)/shard_map/psum | solution.py:181
  89.5 611.5 %all-reduce.8.cloned.1.call-start = ((), (), s32[]{:S(2)}) async-start(), calls=%async_computation.7 | async-start | bytes 16777216 | tf_op jit(solution)/shard_map/psum | solution.py:189
  383.2 7.0 copy-start.8
  383.2 8.2 copy-start.10
  394.7 7.4 copy-start.5
  394.8 9.3 copy-start.36
  411.0 10.2 copy-start.33
  411.0 10.2 copy-start.34
  411.0 10.2 copy-start.35
  411.0 625.0 %all-reduce.10.cloned.1.call-start = ((), (), s32[]{:S(2)}) async-start(), calls=%async_computation.8 | async-start | bytes 16777216 | tf_op jit(solution)/shard_map/psum | solution.py:205
  421.3 287.5 %copy-start.27 = (pred[2048]{0:T(1024)(128)(4,1)}, pred[2048]{0:T(1024)(128)(4,1)S(1)}, u32[]{:S(2)}) copy-start(pred[2048]{0:T(1024)(128)(4,1)S(1)} %iota_compare_fusion.2) | copy-start | bytes 6148
  719.7 6.1 copy-start.7
  719.7 6.1 copy-start.37
  725.8 11.3 copy-start.13
  746.0 549.9 %reduce-scatter.17.cloned.1.call-start = ((), (), s32[]{:S(2)}) async-start(), calls=%async_computation.12 | async-start | bytes 2359296 | tf_op jit(solution)/shard_map/reduce_scatter | solution.py:249
  756.0 541.7 %reduce-scatter.15.cloned.1.call-start = ((), (), s32[]{:S(2)}) async-start(), calls=%async_computation.11 | async-start | bytes 2359296 | tf_op jit(solution)/shard_map/reduce_scatter | solution.py:246
  766.5 578.7 %reduce-scatter.19.cloned.1.call-start = ((), (), s32[]{:S(2)}) async-start(), calls=%async_computation.13 | async-start | bytes 589824
  1052.3 11.8 copy-start.23
  1107.8 7.2 copy-start.2
  1149.3 7.1 copy-start.2
  1190.7 7.2 copy-start.2
  1232.2 7.2 copy-start.2
  1250.3 96.8 %reduce-scatter.21.cloned.1.call-start = ((), (), s32[]{:S(2)}) async-start(), calls=%async_computation.14 | async-start | bytes 589824
  1256.8 100.8 %reduce-scatter.23.cloned.1.call-start = ((), (), s32[]{:S(2)}) async-start(), calls=%async_computation.15 | async-start | bytes 589824
  1261.2 6.8 copy-start.16
  1262.3 10.2 copy-start.18
  1267.9 126.8 %reduce-scatter.13.cloned.1.call-start = ((), (), s32[]{:S(2)}) async-start(), calls=%async_computation.10 | async-start | bytes 589824 | tf_op jit(solution)/shard_map/reduce_scatter | solution.py:243
  1277.0 10.1 copy-start.28
  1277.0 275.0 %all-reduce.12.cloned.1.call-start = ((), (), s32[]{:S(2)}) async-start(), calls=%async_computation.9 | async-start | bytes 8388608 | tf_op jit(solution)/shard_map/psum | solution.py:222
  1286.2 13.3 copy-start.12
  1291.3 264.3 %copy-start.1 = (bf16[1024,1024]{1,0:T(8,128)(2,1)S(1)}, bf16[1024,1024]{1,0:T(8,128)(2,1)}, u32[]{:S(2)}) copy-start(bf16[1024,1024]{1,0:T(8,128)(2,1)} %param.34) | copy-start | bytes 6291460
  (36 other events, 107.0 us)
Sparse Core Ops, SparseCore 0:
  89.6 293.5 all-reduce.5
  411.1 289.7 all-reduce.7
  746.1 289.8 all-reduce.9
  1039.1 40.0 reduce-scatter.16
  1082.4 41.1 reduce-scatter.14
  1250.4 32.5 reduce-scatter.18
  1286.1 34.2 reduce-scatter.20
  1323.4 34.0 reduce-scatter.22
  1360.6 34.0 reduce-scatter.12
  1397.0 154.9 all-reduce.11
where the time goes:
time: 1570 us; the launch traced here: 1560 us
  waiting for transfers between devices  1040 us (66%)
  matrix products  256 us (16%)
  other arithmetic  142 us (9%)
  local copies, waits for them, and re-layouts  53.8 us (3%)
  blocking collectives  49.1 us (3%)
  between operations  18.3 us (1%)
    psum x1, waiting for transfers between devices, shards(): attention_whole = lax.psum(attention_part, 'tensor')  293 us
    psum x1, waiting for transfers between devices, shards(): outer_rows = lax.psum(outer_part, 'tensor')  280 us
    psum x1, waiting for transfers between devices, shards(): normed_back = lax.psum(normed_part, 'tensor')  269 us
    psum x1, waiting for transfers between devices, shards(): lax.psum(input_part.astype(jnp.bfloat16), 'tensor').astype(jnp.float32)  156 us
    convert_element_type x4, other arithmetic, one_block(): score_grad = (probs * (prob_grad - centre)).astype(jnp.bfloat16)  42.8 us
    psum x1, blocking collectives, shards(): lax.psum((placed(jnp.sum(query_low.astype(jnp.float32), axis=0)), placed(...  40.3 us
    dot_general x4, matrix products, one_block(): jnp.einsum('qhd,khd->hqk', grad_block, values_split, preferred_element_ty...  39.8 us
    dot_general x6, matrix products, times_rows(): lax.dot_general(former, latter, (((1,), (1,)), ((), ())), preferred_eleme...  38.7 us
  transfers between devices with their start and end apart: 10, of which 6 were waited for; matrix products, arithmetic and copies ran while one was open for 18% of the time, Pallas kernels for 0%

commit v1 on v0

--- a/solution.py
+++ b/solution.py
@@ -178,7 +178,7 @@
     def take_own(array_in):
         return lax.dynamic_slice_in_dim(array_in, row_start, share_rows, 0)
 
-    attention_whole = lax.psum(attention_part, "tensor")
+    attention_whole = jnp.sum(lax.all_gather(attention_part, "tensor"), axis=0)
     normed, normal_one, inverse_one = layer_norm(
         hidden_float + (attention_whole + output_bias), first_gain, first_shift
     )

time: 1570 us -> 1860 us (1.18)
  waiting for transfers between devices: 1040 us -> 1310 us
    all_gather x0 -> x1, waiting for transfers between devices: none -> 564 us  [shards(): attention_whole = jnp.sum(lax.all_gather(attention_part, 'tensor'), axis=0)]
    psum x1 -> x0, waiting for transfers between devices: 293 us -> none  [shards(): attention_whole = lax.psum(attention_part, 'tensor')]
  transfers between devices with their start and end apart: 10 -> 10, of which waited for: 6 -> 6; matrix products, arithmetic and copies ran while one was open for 18% -> 15% of each run, Pallas kernels for 0% -> 0%
where the time goes in v1:
time: 1860 us; the launch traced here: 1850 us
  waiting for transfers between devices  1310 us (70%)
  matrix products  257 us (14%)
  other arithmetic  157 us (8%)
  local copies, waits for them, and re-layouts  50.9 us (3%)
  blocking collectives  49.6 us (3%)
    all_gather x1, waiting for transfers between devices, shards(): attention_whole = jnp.sum(lax.all_gather(attention_part, 'tensor'), axis=0)  564 us
    psum x1, waiting for transfers between devices, shards(): outer_rows = lax.psum(outer_part, 'tensor')  279 us
    psum x1, waiting for transfers between devices, shards(): normed_back = lax.psum(normed_part, 'tensor')  270 us
    psum x1, waiting for transfers between devices, shards(): lax.psum(input_part.astype(jnp.bfloat16), 'tensor').astype(jnp.float32)  156 us
    convert_element_type x4, other arithmetic, one_block(): score_grad = (probs * (prob_grad - centre)).astype(jnp.bfloat16)  42.8 us
    psum x1, blocking collectives, shards(): lax.psum((placed(jnp.sum(query_low.astype(jnp.float32), axis=0)), placed(...  40.5 us
    dot_general x6, matrix products, times_rows(): lax.dot_general(former, latter, (((1,), (1,)), ((), ())), preferred_eleme...  38.7 us
    dot_general x4, matrix products, one_block(): jnp.einsum('qhd,khd->hqk', grad_block, values_split, preferred_element_ty...  37.5 us
  transfers between devices with their start and end apart: 10, of which 6 were waited for; matrix products, arithmetic and copies ran while one was open for 15% of the time, Pallas kernels for 0%

profile of v1, /device:TPU:0, one launch (start us, length us, event | category | flops | bytes accessed | tf_op | source)
XLA Modules:
  0.0 1847.1 jit_solution(13994985651124538956)
XLA Ops:
  25.3 55.2 %while.28 = (s32[]{:T(128)}, bf16[4,512,4,64]{1,3,2,0:T(8,128)(2,1)}, f32[4,4,512]{2,1,0:T(4,128)}, bf16[4,512,4,64]{1,3,2,0:T(8,128)(2,1)}, bf16[2048,4,64]{0,2...) while((s32[]{:T(128)}, bf16[4,512,4,64]{1,3,2,0:T(8,128)(2,1)}, ...), condition=%wide.region_3.4_spmd.clone, body=%wide.region_0.3_spmd.clone.sunk | while | flops 1124073472 | bytes 65872064 | solution.py:89
  90.3 563.8 %all-gather.3.cloned.1.call-done = f32[8192,1024]{1,0:T(8,128)} async-done(((f32[2048,1024]{1,0:T(8,128)}), f32[8192,1024]{1,0:T(8,128)}) %all-gather.3.cloned.1.call-update) | async-done | bytes 33554448 | tf_op jit(solution)/shard_map/all_gather | solution.py:181
  654.1 16.4 reduce_sum.197
  682.1 7.4 multiply_convert_fusion.1
  698.4 9.1 psum.100
  708.9 278.6 %all-reduce.5.cloned.1.call-done = f32[2048,1024]{1,0:T(8,128)} async-done(((f32[2048,1024]{1,0:T(8,128)}), f32[2048,1024]{1,0:T(8,128)}) %all-reduce.5.cloned.1.call-update) | async-done | bytes 8388624 | tf_op jit(solution)/shard_map/psum | solution.py:189
  995.4 10.9 multiply_reduce_fusion.6
  1012.3 11.4 convert_reduce_fusion
  1025.7 6.9 fusion.72
  1032.8 9.4 convolution_convert_fusion.2
  1042.3 10.5 convolution_convert_fusion.3
  1052.9 269.7 %all-reduce.7.cloned.1.call-done = f32[2048,1024]{1,0:T(8,128)} async-done(((f32[2048,1024]{1,0:T(8,128)}), f32[2048,1024]{1,0:T(8,128)}) %all-reduce.7.cloned.1.call-update) | async-done | bytes 8388624 | tf_op jit(solution)/shard_map/psum | solution.py:205
  1322.6 13.0 multiply_reduce_fusion.5
  1335.7 9.5 fusion.67
  1355.7 169.6 %while.29 = (s32[]{:T(128)}, f32[2048,4,64]{0,2,1:T(8,128)}, f32[2048,4,64]{0,2,1:T(8,128)}, bf16[4,512,4,64]{1,3,2,0:T(8,128)(2,1)}, bf16[4,512,4,64]{1,3,2,0:T...) while((s32[]{:T(128)}, f32[2048,4,64]{0,2,1:T(8,128)}, ...), condition=%wide.region_20.21_spmd.clone, body=%wide.region_18.20_spmd.clone.sunk | while | flops 2750021632 | bytes 172556464 | solution.py:129
  1366.3 9.4 multiply_reduce_fusion.8
  1375.8 11.0 multiply_convert_fusion.3
  1386.7 7.1 fusion.151
  1408.6 9.4 multiply_reduce_fusion.8
  1417.9 10.6 multiply_convert_fusion.3
  1428.6 6.9 fusion.151
  1451.0 9.4 multiply_reduce_fusion.8
  1460.3 10.6 multiply_convert_fusion.3
  1470.9 6.9 fusion.151
  1493.4 9.4 multiply_reduce_fusion.8
  1502.7 10.6 multiply_convert_fusion.3
  1513.3 6.9 fusion.151
  1560.1 9.1 add_convert_fusion
  1587.2 40.5 %all-reduce = (f32[]{:T(128)}, f32[1024]{0:T(1024)}, f32[1024]{0:T(1024)}, f32[1024]{0:T(1024)}, f32[1024]{0:T(1024)}, /*index=5*/f32[1024]{0:T(1024)}, f32[4096...) all-reduce(f32[]{:T(128)} %get-tuple-element.344, ...), channel_id=1, replica_groups=mesh['dp'=8,'tensor'=4] {'dp','tensor'}, use_global_device_ids=true, to_apply=%region_11.12 | all-reduce | flops 12289 | bytes 98312 | tf_op jit(solution)/shard_map/psum | solution.py:260
  1631.8 9.0 reduce-scatter.23.cloned.1.call-done
  1642.5 35.5 %reduce-scatter.13.cloned.1.call-done = bf16[128,256]{1,0:T(8,128)(2,1)} async-done(((bf16[1024,256]{1,0:T(8,128)(2,1)}), bf16[128,256]{1,0:T(8,128)(2,1)}) %reduce-scatter.13.cloned.1.call-update) | async-done | bytes 65552 | tf_op jit(solution)/shard_map/reduce_scatter | solution.py:243
  1679.6 155.7 %all-reduce.9.cloned.1.call-done = bf16[2048,1024]{1,0:T(8,128)(2,1)} async-done(((bf16[2048,1024]{1,0:T(8,128)(2,1)}), bf16[2048,1024]{1,0:T(8,128)(2,1)}) %all-reduce.9.cloned.1.call-update) | async-done | bytes 4194320 | tf_op jit(solution)/shard_map/psum | solution.py:222
  (252 shorter events, 253.6 us)
Async XLA Ops:
  7.2 674.9 %copy-start = (bf16[1024,1024]{1,0:T(8,128)(2,1)S(1)}, bf16[1024,1024]{1,0:T(8,128)(2,1)}, u32[]{:S(2)}) copy-start(bf16[1024,1024]{1,0:T(8,128)(2,1)} %param.34) | copy-start | bytes 6291460
  7.2 646.9 %all-gather.3.cloned.1.call-start = ((), (), s32[]{:S(2)}) async-start(), calls=%async_computation.12 | async-start | bytes 41943040 | tf_op jit(solution)/shard_map/all_gather | solution.py:181
  80.5 9.3 copy-start.3
  89.9 897.6 %all-reduce.5.cloned.1.call-start = ((), (), s32[]{:S(2)}) async-start(), calls=%async_computation.6 | async-start | bytes 16777216 | tf_op jit(solution)/shard_map/psum | solution.py:189
  670.5 7.0 copy-start.6
  670.5 8.2 copy-start.12
  682.1 7.4 copy-start.5
  682.1 9.3 copy-start.39
  698.3 10.5 copy-start.36
  698.3 10.5 copy-start.37
  698.3 10.5 copy-start.38
  698.3 624.2 %all-reduce.7.cloned.1.call-start = ((), (), s32[]{:S(2)}) async-start(), calls=%async_computation.7 | async-start | bytes 16777216 | tf_op jit(solution)/shard_map/psum | solution.py:205
  708.9 286.5 %copy-start.30 = (pred[2048]{0:T(1024)(128)(4,1)}, pred[2048]{0:T(1024)(128)(4,1)S(1)}, u32[]{:S(2)}) copy-start(pred[2048]{0:T(1024)(128)(4,1)S(1)} %iota_compare_fusion.2) | copy-start | bytes 6148
  1012.3 11.4 copy-start.16
  1032.6 546.2 %reduce-scatter.17.cloned.1.call-start = ((), (), s32[]{:S(2)}) async-start(), calls=%async_computation.11 | async-start | bytes 2359296 | tf_op jit(solution)/shard_map/reduce_scatter | solution.py:249
  1042.2 538.3 %reduce-scatter.15.cloned.1.call-start = ((), (), s32[]{:S(2)}) async-start(), calls=%async_computation.10 | async-start | bytes 2359296 | tf_op jit(solution)/shard_map/reduce_scatter | solution.py:246
  1052.8 575.5 %reduce-scatter.19.cloned.1.call-start = ((), (), s32[]{:S(2)}) async-start(), calls=%async_computation.13 | async-start | bytes 589824
  1335.6 9.6 copy-start.10
  1335.6 11.7 copy-start.26
  1345.2 10.5 copy-start.4
  1345.2 10.5 copy-start.14
  1386.7 7.1 copy-start.2
  1470.9 6.9 copy-start.2
  1525.3 8.0 copy-start.9
  1533.2 96.9 %reduce-scatter.21.cloned.1.call-start = ((), (), s32[]{:S(2)}) async-start(), calls=%async_computation.14 | async-start | bytes 589824
  1539.7 101.1 %reduce-scatter.23.cloned.1.call-start = ((), (), s32[]{:S(2)}) async-start(), calls=%async_computation.15 | async-start | bytes 589824
  1545.2 10.3 copy-start.21
  1550.9 127.1 %reduce-scatter.13.cloned.1.call-start = ((), (), s32[]{:S(2)}) async-start(), calls=%async_computation.9 | async-start | bytes 589824 | tf_op jit(solution)/shard_map/reduce_scatter | solution.py:243
  1560.0 10.1 copy-start.31
  1560.1 275.3 %all-reduce.9.cloned.1.call-start = ((), (), s32[]{:S(2)}) async-start(), calls=%async_computation.8 | async-start | bytes 8388608 | tf_op jit(solution)/shard_map/psum | solution.py:222
  1569.2 13.2 copy-start.15
  1574.2 264.7 %copy-start.1 = (bf16[1024,1024]{1,0:T(8,128)(2,1)S(1)}, bf16[1024,1024]{1,0:T(8,128)(2,1)}, u32[]{:S(2)}) copy-start(bf16[1024,1024]{1,0:T(8,128)(2,1)} %param.34) | copy-start | bytes 6291460
  (33 other events, 124.8 us)
Sparse Core Ops, SparseCore 0:
  90.0 564.0 all-gather.2
  698.4 289.0 all-reduce.4
  1032.7 289.7 all-reduce.6
  1325.7 40.0 reduce-scatter.16
  1369.0 41.1 reduce-scatter.14
  1533.3 32.8 reduce-scatter.18
  1569.3 34.2 reduce-scatter.20
  1606.6 34.1 reduce-scatter.22
  1643.9 34.1 reduce-scatter.12
  1680.3 154.9 all-reduce.8
